TPU v7x, 512 devices: a whole 4x4x16 slice. The times are simulated.
512 devices in a mesh: mesh: 64 (over y, z), obs: 8 (over x, core).
Axes of the slice: x: 4, y: 4, z: 16, core: 2. Of those that a mesh axis runs over, the one named last changes fastest.
Arguments:
- probes: bfloat16 [64, 512, 2048], P(None, 'mesh', 'obs'), may hold values from -6 to 6
- velocity: float32 [512, 2048], P('mesh', 'obs'), may hold values from 0.5 to 2
- viscosity: float32 [512, 2048], P('mesh', 'obs'), may hold values from 0.1 to 3
- friction: float32 [512, 2048], P('mesh', 'obs'), may hold values from 0.5 to 4
- obs_block: int32 [64, 512], P('mesh', 'obs'), may hold values from 0 to 127
- obs_weight: float32 [64, 512, 128], P('mesh', 'obs'), may hold values from -0.5 to 0.5
- obs_prec: float32 [64, 512], P('mesh', 'obs'), may hold values from 0.05 to 0.5
- rank: int32 [1], replicated, may hold values from 1 to 64
Outputs:
- basis: float32 [64, 512, 2048], P(None, 'mesh', 'obs')
- factor: float32 [64, 64], replicated
All inputs are finite; a program needn't handle non-finite values.
Results may differ from a plain program's by a relative error of at most 0.0027.
Values may be sent and summed in bfloat16 or wider, within the bound.
A program may use at most 64 MiB of HBM per device.

v0:
```python
import jax
import jax.numpy as jnp
from jax import lax
from jax.sharding import PartitionSpec as P

BLOCK = 128
PRIOR = 1.0


def extended(block, sides, width):
    for axis, dim in sides:
        count = lax.axis_size(axis)
        forward = [(i, i + 1) for i in range(count - 1)]
        backward = [(target, source) for source, target in forward]
        low = lax.ppermute(
            lax.slice_in_dim(block, block.shape[dim] - width, None, axis=dim), axis, forward
        )
        high = lax.ppermute(lax.slice_in_dim(block, 0, width, axis=dim), axis, backward)
        block = jnp.concatenate([low, block, high], axis=dim)
    return block


def apply_padded(padded, visc_pad, friction):
    height = padded.shape[1] - 2
    width = padded.shape[2] - 2
    centre = padded[:, 1:-1, 1:-1]
    visc_mid = visc_pad[1:-1, 1:-1]
    result = friction * centre
    for shift_row, shift_col in ((2, 1), (0, 1), (1, 2), (1, 0)):
        neighbor = padded[:, shift_row : shift_row + height, shift_col : shift_col + width]
        face_coef = 0.5 * (
            visc_mid + visc_pad[shift_row : shift_row + height, shift_col : shift_col + width]
        )
        result = result + face_coef * (centre - neighbor)
    return result


def per_device(probes, velocity, viscosity, friction, obs_block, obs_weight, obs_prec, rank):
    probe_count = probes.shape[0]
    rows_here, cols_here = velocity.shape
    obs_devices = lax.axis_size("obs")
    slab_columns = cols_here * obs_devices // BLOCK
    owned_blocks = cols_here // BLOCK
    cell_total = rows_here * cols_here * lax.axis_size("mesh") * obs_devices
    omega = probes.astype(jnp.float32)
    stacked = jnp.concatenate([velocity[None] * omega, viscosity[None]], axis=0)
    padded = extended(stacked, (("mesh", 1), ("obs", 2)), 1)
    visc_pad = padded[-1]
    tangent = apply_padded(padded[:-1], visc_pad, friction).astype(jnp.bfloat16)
    row_ids = obs_block[0] // slab_columns
    col_ids = obs_block[0] % slab_columns
    weights = obs_weight[0]
    precision = obs_prec[0]
    segment = lax.all_gather(tangent, "obs", axis=2, tiled=True)
    seg_blocks = segment.shape[2] // BLOCK
    local_col = col_ids
    inside = (local_col >= 0) & (local_col < seg_blocks)
    block_index = row_ids * seg_blocks + jnp.clip(local_col, 0, seg_blocks - 1)
    blocks = segment.reshape(probe_count, rows_here * seg_blocks, BLOCK)
    picked = jnp.take(blocks, block_index, axis=1).astype(jnp.float32)
    value = precision * jnp.sum(picked * weights, axis=-1)
    misfit = jnp.where(inside, value, 0.0)
    amount = lax.axis_size("obs") * owned_blocks
    local_col = col_ids
    inside = (local_col >= 0) & (local_col < amount)
    block_index = jnp.clip(local_col, 0, amount - 1) * rows_here + row_ids
    contrib = jnp.where(inside[None, :, None], misfit[:, :, None] * weights[None], 0.0)
    partial_value = (
        jnp.zeros((probe_count, amount * rows_here, BLOCK), jnp.float32)
        .at[:, block_index]
        .add(contrib)
    )
    received = lax.psum_scatter(
        partial_value.reshape(probe_count, amount, rows_here, BLOCK).transpose(1, 0, 2, 3),
        "obs",
        scatter_dimension=0,
        tiled=True,
    )
    source = received.transpose(1, 2, 0, 3).reshape(probe_count, rows_here, cols_here)
    padded_source = extended(source, (("mesh", 1), ("obs", 2)), 1)
    gradient = velocity * apply_padded(padded_source, visc_pad, friction)
    sketch = (gradient + PRIOR * omega).reshape(probe_count, rows_here * cols_here)
    local_gram = (
        jnp.dot(
            sketch, sketch.T, precision=lax.Precision.HIGHEST, preferred_element_type=jnp.float32
        )
        / cell_total
    )
    factor = jnp.linalg.cholesky(lax.psum(local_gram, ("mesh", "obs")))
    solved = lax.linalg.triangular_solve(factor, sketch, left_side=True, lower=True)
    retained = (jnp.arange(probe_count, dtype=jnp.int32) < rank[0])[:, None]
    basis = jnp.where(retained, solved, 0.0).reshape(probe_count, rows_here, cols_here)
    return (basis, factor)


def solution(mesh):
    in_specs = (
        P(None, "mesh", "obs"),
        P("mesh", "obs"),
        P("mesh", "obs"),
        P("mesh", "obs"),
        P("mesh", "obs"),
        P("mesh", "obs", None),
        P("mesh", "obs"),
        P(),
    )
    out_specs = (P(None, "mesh", "obs"), P())
    return jax.shard_map(
        per_device, mesh=mesh, in_specs=in_specs, out_specs=out_specs, check_vma=False
    )
```

profile of v0, /device:TPU:1, one launch (start us, length us, event | category | flops | bytes accessed | tf_op | source)
XLA Modules:
  0.0 289.0 jit_solution(15032128486639405339)
XLA Ops:
  9.1 4.4 %collective-permute-start = (f32[65,1,256]{2,0,1:T(8,128)S(1)}, f32[65,1,256]{2,0,1:T(8,128)S(1)}, u32[]{:S(2)}, u32[]{:S(2)}) collective-permute-start(f32[65,1,256]{2,0,1:T(8,128)S(1)} %copy.38), channel_id=1, source_target_pairs={{0,8},{8,16},{16,24},{24,32},{32,40},{40,48},{48,56},{56,64},{64,7... | collective-permute-start | bytes 199688 | tf_op jit(solution)/shard_map/ppermute | solution.py:15
  13.5 1.3 collective-permute-start.1
  14.9 3.8 %collective-permute-done.1 = f32[65,1,256]{2,0,1:T(8,128)S(1)} collective-permute-done((f32[65,1,256]{2,0,1:T(8,128)S(1)}, f32[65,1,256]{2,0,1:T(8,128)S(1)}, u32[]{:S(2)}, u32[]{:S(2)}) %collective-permute-start.1) | collective-permute-done | bytes 66592 | tf_op jit(solution)/shard_map/ppermute | solution.py:18
  20.2 4.9 %collective-permute-start.2 = (f32[65,10,1]{0,1,2:T(8,128)S(1)}, f32[65,10,1]{0,1,2:T(8,128)S(1)}, u32[]{:S(2)}, u32[]{:S(2)}) collective-permute-start(f32[65,10,1]{0,1,2:T(8,128)S(1)} %copy.42), channel_id=1, source_target_pairs={{0,1},{1,2},{2,3},{3,4},{4,5},{5,6},{6,7},{8,9},{9,10},{10,11},{11... | collective-permute-start | bytes 7808 | tf_op jit(solution)/shard_map/ppermute | solution.py:15
  25.4 3.0 %collective-permute-start.3 = (f32[65,10,1]{0,1,2:T(8,128)S(1)}, f32[65,10,1]{0,1,2:T(8,128)S(1)}, u32[]{:S(2)}, u32[]{:S(2)}) collective-permute-start(f32[65,10,1]{0,1,2:T(8,128)S(1)} %copy.43), channel_id=1, source_target_pairs={{1,0},{2,1},{3,2},{4,3},{5,4},{6,5},{7,6},{9,8},{10,9},{11,10},{12... | collective-permute-start | bytes 7808 | tf_op jit(solution)/shard_map/ppermute | solution.py:18
  28.8 1.6 collective-permute-done.3
  30.9 1.8 fusion.17
  32.9 38.9 %all-gather.2.cloned.1.call-done = bf16[64,8,2048]{2,1,0:T(8,128)(2,1)} async-done(((bf16[64,8,256]{2,1,0:T(8,128)(2,1)}), bf16[64,8,2048]{2,1,0:T(8,128)(2,1)}) %all-gather.2.cloned.1.call-update) | async-done | bytes 2097168 | tf_op jit(solution)/shard_map/all_gather | solution.py:54
  71.7 2.9 reshape.238
  74.6 2.7 copy.50
  77.3 2.3 gather_fusion
  81.4 2.5 broadcast_in_dim.67
  83.9 9.0 %scatter_fusion = f32[64,128,128]{2,0,1:T(8,128)} fusion(f32[64,128,128]{2,0,1:T(8,128)} %broadcast_in_dim.67, s32[64]{0:T(128)S(1)} %fusion.36, f32[64,64,128]{2,1,0:T(8,128)S(1)} %select_bitcast_fusion), kind=kCustom, calls=%fused_computation.1 | custom fusion | flops 524288 | bytes 6291712 | tf_op jit(solution)/shard_map/scatter-add | solution.py:71
  92.9 44.1 %reduce-scatter.2.cloned.1.call-done = f32[2,64,8,128]{3,1,2,0:T(8,128)} async-done(((f32[16,64,8,128]{3,1,2,0:T(8,128)}), f32[2,64,8,128]{3,1,2,0:T(8,128)}) %reduce-scatter.2.cloned.1.call-update) | async-done | bytes 524304 | tf_op jit(solution)/shard_map/reduce_scatter | solution.py:73
  137.0 1.3 copy.63
  138.5 1.3 collective-permute-start.4
  139.8 4.0 %collective-permute-start.5 = (f32[64,1,256]{2,1,0:T(1,128)S(1)}, f32[64,1,256]{2,1,0:T(1,128)S(1)}, u32[]{:S(2)}, u32[]{:S(2)}) collective-permute-start(f32[64,1,256]{2,1,0:T(1,128)S(1)} %get-tuple-element.13), channel_id=1, source_target_pairs={{0,8},{8,16},{16,24},{24,32},{32,40},{40,48},{48,56},{56,64},{64,7... | collective-permute-start | bytes 196616 | tf_op jit(solution)/shard_map/ppermute | solution.py:15
  145.5 6.2 %collective-permute-start.6 = (f32[64,10,1]{2,1,0:T(8,128)S(1)}, f32[64,10,1]{2,1,0:T(8,128)S(1)}, u32[]{:S(2)}, u32[]{:S(2)}) collective-permute-start(f32[64,10,1]{2,1,0:T(8,128)S(1)} %get-tuple-element.9), channel_id=1, source_target_pairs={{1,0},{2,1},{3,2},{4,3},{5,4},{6,5},{7,6},{9,8},{10,9},{11,10},{12... | collective-permute-start | bytes 7688 | tf_op jit(solution)/shard_map/ppermute | solution.py:18
  151.6 1.9 collective-permute-start.7
  153.6 2.5 collective-permute-done.6
  156.1 3.6 %collective-permute-done.7 = f32[64,10,1]{2,1,0:T(8,128)S(1)} collective-permute-done((f32[64,10,1]{2,1,0:T(8,128)S(1)}, f32[64,10,1]{2,1,0:T(8,128)S(1)}, u32[]{:S(2)}, u32[]{:S(2)}) %collective-permute-start.7) | collective-permute-done | bytes 2592 | tf_op jit(solution)/shard_map/ppermute | solution.py:15
  161.2 106.3 %psum.7 = f32[64,64]{0,1:T(8,128)S(1)} all-reduce(f32[64,64]{0,1:T(8,128)S(1)} %fusion), channel_id=1, replica_groups=mesh['mesh'=64,'obs'=8] {'mesh','obs'}, use_global_device_ids=true, to_apply=%region_3.4 | all-reduce | flops 4096 | bytes 32768 | tf_op jit(solution)/shard_map/psum | solution.py:89
  267.7 5.8 %cholesky.15 = f32[64,64]{1,0:T(8,128)S(1)} custom-call(f32[64,64]{1,0:T(8,128)S(1)} %fusion.29), custom_call_target="Cholesky" | custom-call | tf_op jit(solution)/shard_map/jit(cholesky)/cholesky | solution.py:89
  275.4 4.9 %custom-call.6 = f32[1,64,64]{1,2,0:T(8,128)S(1)} custom-call(f32[1,64,64]{2,1,0:T(8,128)S(1)} %get-tuple-element.2), custom_call_target="InvertDiagBlocksLowerTriangular" | custom-call | tf_op jit(solution)/shard_map/triangular_solve | solution.py:90
  (57 shorter events, 12.9 us)
Async XLA Ops:
  7.2 64.5 %all-gather.2.cloned.1.call-start = ((), (), s32[]{:S(2)}) async-start(), calls=%async_computation.1 | async-start | bytes 2359296 | tf_op jit(solution)/shard_map/all_gather | solution.py:54
  9.1 5.8 %collective-permute-start = (f32[65,1,256]{2,0,1:T(8,128)S(1)}, f32[65,1,256]{2,0,1:T(8,128)S(1)}, u32[]{:S(2)}, u32[]{:S(2)}) collective-permute-start(f32[65,1,256]{2,0,1:T(8,128)S(1)} %copy.38), channel_id=1, source_target_pairs={{0,8},{8,16},{16,24},{24,32},{32,40},{40,48},{48,56},{56,64},{64,7... | collective-permute-start | bytes 199688 | tf_op jit(solution)/shard_map/ppermute | solution.py:15
  13.5 5.3 %collective-permute-start.1 = (f32[65,1,256]{2,0,1:T(8,128)S(1)}, f32[65,1,256]{2,0,1:T(8,128)S(1)}, u32[]{:S(2)}, u32[]{:S(2)}) collective-permute-start(f32[65,1,256]{2,0,1:T(8,128)S(1)} %copy.39), channel_id=1, source_target_pairs={{8,0},{16,8},{24,16},{32,24},{40,32},{48,40},{56,48},{64,56},{72,6... | collective-permute-start | bytes 199688 | tf_op jit(solution)/shard_map/ppermute | solution.py:18
  19.7 11.0 %copy-start.2 = (f32[8,256]{1,0:T(8,128)S(1)}, f32[8,256]{1,0:T(8,128)}, u32[]{:S(2)}) copy-start(f32[8,256]{1,0:T(8,128)} %param.10) | copy-start | bytes 24580
  19.9 11.0 %copy-start.4 = (f32[8,256]{1,0:T(8,128)S(1)}, f32[8,256]{1,0:T(8,128)}, u32[]{:S(2)}) copy-start(f32[8,256]{1,0:T(8,128)} %param.11) | copy-start | bytes 24580
  20.2 8.2 %collective-permute-start.2 = (f32[65,10,1]{0,1,2:T(8,128)S(1)}, f32[65,10,1]{0,1,2:T(8,128)S(1)}, u32[]{:S(2)}, u32[]{:S(2)}) collective-permute-start(f32[65,10,1]{0,1,2:T(8,128)S(1)} %copy.42), channel_id=1, source_target_pairs={{0,1},{1,2},{2,3},{3,4},{4,5},{5,6},{6,7},{8,9},{9,10},{10,11},{11... | collective-permute-start | bytes 7808 | tf_op jit(solution)/shard_map/ppermute | solution.py:15
  25.4 5.0 %collective-permute-start.3 = (f32[65,10,1]{0,1,2:T(8,128)S(1)}, f32[65,10,1]{0,1,2:T(8,128)S(1)}, u32[]{:S(2)}, u32[]{:S(2)}) collective-permute-start(f32[65,10,1]{0,1,2:T(8,128)S(1)} %copy.43), channel_id=1, source_target_pairs={{1,0},{2,1},{3,2},{4,3},{5,4},{6,5},{7,6},{9,8},{10,9},{11,10},{12... | collective-permute-start | bytes 7808 | tf_op jit(solution)/shard_map/ppermute | solution.py:18
  30.8 2.0 copy-start.6
  32.7 104.3 %reduce-scatter.2.cloned.1.call-start = ((), (), s32[]{:S(2)}) async-start(), calls=%async_computation.2 | async-start | bytes 4718592 | tf_op jit(solution)/shard_map/reduce_scatter | solution.py:73
  77.3 2.4 copy-start.1
  77.3 3.2 %copy-start.5 = (f32[1,64]{1,0:T(1,128)S(1)}, f32[1,64]{1,0:T(1,128)}, u32[]{:S(2)}) copy-start(f32[1,64]{1,0:T(1,128)} %param.14) | copy-start | bytes 772
  138.3 21.3 %copy-start = (bf16[64,8,256]{2,1,0:T(8,128)(2,1)S(1)}, bf16[64,8,256]{2,1,0:T(8,128)(2,1)}, u32[]{:S(2)}) copy-start(bf16[64,8,256]{2,1,0:T(8,128)(2,1)} %param.8) | copy-start | bytes 786436
  138.4 21.3 %copy-start.3 = (f32[8,256]{1,0:T(8,128)S(1)}, f32[8,256]{1,0:T(8,128)}, u32[]{:S(2)}) copy-start(f32[8,256]{1,0:T(8,128)} %param.9) | copy-start | bytes 24580
  138.5 5.9 %collective-permute-start.4 = (f32[64,1,256]{2,1,0:T(1,128)S(1)}, f32[64,1,256]{2,1,0:T(1,128)S(1)}, u32[]{:S(2)}, u32[]{:S(2)}) collective-permute-start(f32[64,1,256]{2,1,0:T(1,128)S(1)} %get-tuple-element.14), channel_id=1, source_target_pairs={{8,0},{16,8},{24,16},{32,24},{40,32},{48,40},{56,48},{64,56},{72,6... | collective-permute-start | bytes 196616 | tf_op jit(solution)/shard_map/ppermute | solution.py:18
  139.8 5.3 %collective-permute-start.5 = (f32[64,1,256]{2,1,0:T(1,128)S(1)}, f32[64,1,256]{2,1,0:T(1,128)S(1)}, u32[]{:S(2)}, u32[]{:S(2)}) collective-permute-start(f32[64,1,256]{2,1,0:T(1,128)S(1)} %get-tuple-element.13), channel_id=1, source_target_pairs={{0,8},{8,16},{16,24},{24,32},{32,40},{40,48},{48,56},{56,64},{64,7... | collective-permute-start | bytes 196616 | tf_op jit(solution)/shard_map/ppermute | solution.py:15
  145.5 10.6 %collective-permute-start.6 = (f32[64,10,1]{2,1,0:T(8,128)S(1)}, f32[64,10,1]{2,1,0:T(8,128)S(1)}, u32[]{:S(2)}, u32[]{:S(2)}) collective-permute-start(f32[64,10,1]{2,1,0:T(8,128)S(1)} %get-tuple-element.9), channel_id=1, source_target_pairs={{1,0},{2,1},{3,2},{4,3},{5,4},{6,5},{7,6},{9,8},{10,9},{11,10},{12... | collective-permute-start | bytes 7688 | tf_op jit(solution)/shard_map/ppermute | solution.py:18
  151.6 8.0 %collective-permute-start.7 = (f32[64,10,1]{2,1,0:T(8,128)S(1)}, f32[64,10,1]{2,1,0:T(8,128)S(1)}, u32[]{:S(2)}, u32[]{:S(2)}) collective-permute-start(f32[64,10,1]{2,1,0:T(8,128)S(1)} %get-tuple-element.10), channel_id=1, source_target_pairs={{0,1},{1,2},{2,3},{3,4},{4,5},{5,6},{6,7},{8,9},{9,10},{10,11},{11... | collective-permute-start | bytes 7688 | tf_op jit(solution)/shard_map/ppermute | solution.py:15
Sparse Core Ops, SparseCore 0:
  32.8 38.8 all-gather.1
  93.0 43.9 reduce-scatter.1
where the time goes:
time: 290 us; the launch traced here: 289 us
  blocking collectives  106 us (37%)
  waiting for transfers between devices  95.2 us (33%)
  other arithmetic  29.1 us (10%)
  starting transfers between devices  27 us (9%)
  between operations  15 us (5%)
  local copies, waits for them, and re-layouts  14.9 us (5%)
    psum x1, blocking collectives, per_device(): factor = jnp.linalg.cholesky(lax.psum(local_gram, ('mesh', 'obs')))  106 us
    reduce_scatter x1, waiting for transfers between devices, per_device(): lax.psum_scatter(partial_value.reshape(probe_count, amount, rows_here, BL...  44.1 us
    all_gather x1, waiting for transfers between devices, per_device(): segment = lax.all_gather(tangent, 'obs', axis=2, tiled=True)  38.9 us
    ppermute x4, starting transfers between devices, extended(): lax.ppermute(lax.slice_in_dim(block, block.shape[dim] - width, None, axis...  15.2 us
    ppermute x4, starting transfers between devices, extended(): lax.ppermute(lax.slice_in_dim(block, 0, width, axis=dim), axis, backward)  11.8 us
    scatter-add x1, other arithmetic, per_device(): partial_value = jnp.zeros((probe_count, amount * rows_here, BLOCK), jnp.f...  9.02 us
    ppermute x4, waiting for transfers between devices, extended(): lax.ppermute(lax.slice_in_dim(block, 0, width, axis=dim), axis, backward)  7.92 us
    another operation x3, other arithmetic, per_device(): factor = jnp.linalg.cholesky(lax.psum(local_gram, ('mesh', 'obs')))  6.52 us
  transfers between devices with their start and end apart: 10, of which 8 were waited for; matrix products, arithmetic and copies ran while one was open for 0% of the time, Pallas kernels for 0%

commit v1 on v0

--- a/solution.py
+++ b/solution.py
@@ -51,7 +51,9 @@
     col_ids = obs_block[0] % slab_columns
     weights = obs_weight[0]
     precision = obs_prec[0]
-    segment = lax.all_gather(tangent, "obs", axis=2, tiled=True)
+    segment = jnp.concatenate(
+        lax.all_to_all(jnp.stack([tangent] * lax.axis_size("obs")), "obs", 0, 0), axis=2
+    )
     seg_blocks = segment.shape[2] // BLOCK
     local_col = col_ids
     inside = (local_col >= 0) & (local_col < seg_blocks)

time: 290 us -> 288 us (level)
  waiting for transfers between devices: 95.2 us -> 84.5 us
  local copies, waits for them, and re-layouts: 14.9 us -> 19.7 us
  starting transfers between devices: 27 us -> 31.1 us
    all_gather x1 -> x0, waiting for transfers between devices: 38.9 us -> none  [per_device(): segment = lax.all_gather(tangent, 'obs', axis=2, tiled=True)]
    all_to_all x0 -> x1, waiting for transfers between devices: none -> 26.3 us  [per_device(): lax.all_to_all(jnp.stack([tangent] * lax.axis_size('obs')), 'obs', 0, 0)]
    another operation x0 -> x3, local copies, waits for them, and re-layouts: none -> 6.83 us  [the longest x2 5.36 us: per_device(): blocks = segment.reshape(probe_count, rows_here * seg_blocks, BLOCK)]
    all_to_all x0 -> x1, starting transfers between devices: none -> 4.25 us  [per_device(): lax.all_to_all(jnp.stack([tangent] * lax.axis_size('obs')), 'obs', 0, 0)]
where the time goes in v1:
time: 288 us; the launch traced here: 287 us
  blocking collectives  106 us (37%)
  waiting for transfers between devices  84.5 us (29%)
  starting transfers between devices  31.1 us (11%)
  other arithmetic  28.5 us (10%)
  local copies, waits for them, and re-layouts  19.7 us (7%)
  between operations  15 us (5%)
    psum x1, blocking collectives, per_device(): factor = jnp.linalg.cholesky(lax.psum(local_gram, ('mesh', 'obs')))  106 us
    reduce_scatter x1, waiting for transfers between devices, per_device(): lax.psum_scatter(partial_value.reshape(probe_count, amount, rows_here, BL...  46.2 us
    all_to_all x1, waiting for transfers between devices, per_device(): lax.all_to_all(jnp.stack([tangent] * lax.axis_size('obs')), 'obs', 0, 0)  26.3 us
    ppermute x4, starting transfers between devices, extended(): lax.ppermute(lax.slice_in_dim(block, block.shape[dim] - width, None, axis...  15.4 us
    ppermute x4, starting transfers between devices, extended(): lax.ppermute(lax.slice_in_dim(block, 0, width, axis=dim), axis, backward)  11.5 us
    scatter-add x1, other arithmetic, per_device(): partial_value = jnp.zeros((probe_count, amount * rows_here, BLOCK), jnp.f...  9.15 us
    ppermute x4, waiting for transfers between devices, extended(): lax.ppermute(lax.slice_in_dim(block, 0, width, axis=dim), axis, backward)  7.89 us
    another operation x3, other arithmetic, per_device(): factor = jnp.linalg.cholesky(lax.psum(local_gram, ('mesh', 'obs')))  6.52 us
  transfers between devices with their start and end apart: 10, of which 8 were waited for; matrix products, arithmetic and copies ran while one was open for 0% of the time, Pallas kernels for 0%

profile of v1, /device:TPU:1, one launch (start us, length us, event | category | flops | bytes accessed | tf_op | source)
XLA Modules:
  0.0 286.6 jit_solution(17486667626108287922)
XLA Ops:
  9.0 4.4 %collective-permute-start = (f32[65,1,256]{2,0,1:T(8,128)S(1)}, f32[65,1,256]{2,0,1:T(8,128)S(1)}, u32[]{:S(2)}, u32[]{:S(2)}) collective-permute-start(f32[65,1,256]{2,0,1:T(8,128)S(1)} %copy.34), channel_id=1, source_target_pairs={{0,8},{8,16},{16,24},{24,32},{32,40},{40,48},{48,56},{56,64},{64,7... | collective-permute-start | bytes 199688 | tf_op jit(solution)/shard_map/ppermute | solution.py:15
  14.9 3.8 %collective-permute-done.1 = f32[65,1,256]{2,0,1:T(8,128)S(1)} collective-permute-done((f32[65,1,256]{2,0,1:T(8,128)S(1)}, f32[65,1,256]{2,0,1:T(8,128)S(1)}, u32[]{:S(2)}, u32[]{:S(2)}) %collective-permute-start.1) | collective-permute-done | bytes 66592 | tf_op jit(solution)/shard_map/ppermute | solution.py:18
  20.2 4.9 %collective-permute-start.2 = (f32[65,10,1]{0,1,2:T(8,128)S(1)}, f32[65,10,1]{0,1,2:T(8,128)S(1)}, u32[]{:S(2)}, u32[]{:S(2)}) collective-permute-start(f32[65,10,1]{0,1,2:T(8,128)S(1)} %copy.38), channel_id=1, source_target_pairs={{0,1},{1,2},{2,3},{3,4},{4,5},{5,6},{6,7},{8,9},{9,10},{10,11},{11... | collective-permute-start | bytes 7808 | tf_op jit(solution)/shard_map/ppermute | solution.py:15
  25.4 3.0 %collective-permute-start.3 = (f32[65,10,1]{0,1,2:T(8,128)S(1)}, f32[65,10,1]{0,1,2:T(8,128)S(1)}, u32[]{:S(2)}, u32[]{:S(2)}) collective-permute-start(f32[65,10,1]{0,1,2:T(8,128)S(1)} %copy.39), channel_id=1, source_target_pairs={{1,0},{2,1},{3,2},{4,3},{5,4},{6,5},{7,6},{9,8},{10,9},{11,10},{12... | collective-permute-start | bytes 7808 | tf_op jit(solution)/shard_map/ppermute | solution.py:18
  28.8 1.6 collective-permute-done.3
  31.9 1.5 stack.2
  33.4 4.2 %all-to-all-start = ((bf16[8,64,8,256]{3,2,1,0:T(8,128)(2,1)}), bf16[8,64,8,256]{3,2,1,0:T(8,128)(2,1)S(1)}, u32[]{:S(2)}, u32[]{:S(2)}) async-start(bf16[8,64,8,256]{3,2,1,0:T(8,128)(2,1)} %stack.2), calls=%async_computation | async-start | bytes 4194304 | tf_op jit(solution)/shard_map/all_to_all | solution.py:55
  37.7 26.3 %all-to-all-done = bf16[8,64,8,256]{3,2,1,0:T(8,128)(2,1)S(1)} async-done(((bf16[8,64,8,256]{3,2,1,0:T(8,128)(2,1)}), bf16[8,64,8,256]{3,2,1,0:T(8,128)(2,1)S(1)}, u32[]{:S(2)}, u32[]{:S(2)}) %all-to-all-start) | async-done | bytes 2097184 | tf_op jit(solution)/shard_map/all_to_all | solution.py:55
  64.0 3.6 %copy.46 = bf16[64,8,8,256]{3,2,1,0:T(8,128)(2,1)} copy(bf16[64,8,8,256]{3,1,0,2:T(8,128)(2,1)S(1)} %bitcast.78) | data formatting | bytes 4194304 | tf_op jit(solution)/shard_map/reshape | solution.py:54
  67.6 2.7 reshape_reshape.3
  70.3 2.7 copy.47
  72.9 2.3 gather_fusion
  77.0 2.5 broadcast_in_dim.67
  79.5 9.1 %scatter_fusion = f32[64,128,128]{2,0,1:T(8,128)} fusion(f32[64,128,128]{2,0,1:T(8,128)} %broadcast_in_dim.67, s32[64]{0:T(128)S(1)} %fusion.36, f32[64,64,128]{2,1,0:T(8,128)S(1)} %select_bitcast_fusion), kind=kCustom, calls=%fused_computation.1 | custom fusion | flops 524288 | bytes 6291712 | tf_op jit(solution)/shard_map/scatter-add | solution.py:73
  88.7 46.2 %reduce-scatter.2.cloned.1.call-done = f32[2,64,8,128]{3,1,2,0:T(8,128)} async-done(((f32[16,64,8,128]{3,1,2,0:T(8,128)}), f32[2,64,8,128]{3,1,2,0:T(8,128)}) %reduce-scatter.2.cloned.1.call-update) | async-done | bytes 524304 | tf_op jit(solution)/shard_map/reduce_scatter | solution.py:75
  134.9 1.3 copy.60
  137.6 4.0 %collective-permute-start.5 = (f32[64,1,256]{2,1,0:T(1,128)S(1)}, f32[64,1,256]{2,1,0:T(1,128)S(1)}, u32[]{:S(2)}, u32[]{:S(2)}) collective-permute-start(f32[64,1,256]{2,1,0:T(1,128)S(1)} %get-tuple-element.13), channel_id=1, source_target_pairs={{0,8},{8,16},{16,24},{24,32},{32,40},{40,48},{48,56},{56,64},{64,7... | collective-permute-start | bytes 196616 | tf_op jit(solution)/shard_map/ppermute | solution.py:15
  143.3 5.9 %collective-permute-start.6 = (f32[64,10,1]{2,1,0:T(8,128)S(1)}, f32[64,10,1]{2,1,0:T(8,128)S(1)}, u32[]{:S(2)}, u32[]{:S(2)}) collective-permute-start(f32[64,10,1]{2,1,0:T(8,128)S(1)} %get-tuple-element.9), channel_id=1, source_target_pairs={{1,0},{2,1},{3,2},{4,3},{5,4},{6,5},{7,6},{9,8},{10,9},{11,10},{12... | collective-permute-start | bytes 7688 | tf_op jit(solution)/shard_map/ppermute | solution.py:18
  149.2 2.1 collective-permute-start.7
  151.3 2.5 collective-permute-done.6
  153.8 3.4 %collective-permute-done.7 = f32[64,10,1]{2,1,0:T(8,128)S(1)} collective-permute-done((f32[64,10,1]{2,1,0:T(8,128)S(1)}, f32[64,10,1]{2,1,0:T(8,128)S(1)}, u32[]{:S(2)}, u32[]{:S(2)}) %collective-permute-start.7) | collective-permute-done | bytes 2592 | tf_op jit(solution)/shard_map/ppermute | solution.py:15
  158.8 106.4 %psum.7 = f32[64,64]{0,1:T(8,128)S(1)} all-reduce(f32[64,64]{0,1:T(8,128)S(1)} %fusion), channel_id=1, replica_groups=mesh['mesh'=64,'obs'=8] {'mesh','obs'}, use_global_device_ids=true, to_apply=%region_3.4 | all-reduce | flops 4096 | bytes 32768 | tf_op jit(solution)/shard_map/psum | solution.py:91
  265.3 5.8 %cholesky.15 = f32[64,64]{1,0:T(8,128)S(1)} custom-call(f32[64,64]{1,0:T(8,128)S(1)} %fusion.29), custom_call_target="Cholesky" | custom-call | tf_op jit(solution)/shard_map/jit(cholesky)/cholesky | solution.py:91
  273.1 4.9 %custom-call.6 = f32[1,64,64]{1,2,0:T(8,128)S(1)} custom-call(f32[1,64,64]{2,1,0:T(8,128)S(1)} %get-tuple-element.2), custom_call_target="InvertDiagBlocksLowerTriangular" | custom-call | tf_op jit(solution)/shard_map/triangular_solve | solution.py:92
  (58 shorter events, 16.5 us)
Async XLA Ops:
  9.0 5.8 %collective-permute-start = (f32[65,1,256]{2,0,1:T(8,128)S(1)}, f32[65,1,256]{2,0,1:T(8,128)S(1)}, u32[]{:S(2)}, u32[]{:S(2)}) collective-permute-start(f32[65,1,256]{2,0,1:T(8,128)S(1)} %copy.34), channel_id=1, source_target_pairs={{0,8},{8,16},{16,24},{24,32},{32,40},{40,48},{48,56},{56,64},{64,7... | collective-permute-start | bytes 199688 | tf_op jit(solution)/shard_map/ppermute | solution.py:15
  13.4 5.3 %collective-permute-start.1 = (f32[65,1,256]{2,0,1:T(8,128)S(1)}, f32[65,1,256]{2,0,1:T(8,128)S(1)}, u32[]{:S(2)}, u32[]{:S(2)}) collective-permute-start(f32[65,1,256]{2,0,1:T(8,128)S(1)} %copy.35), channel_id=1, source_target_pairs={{8,0},{16,8},{24,16},{32,24},{40,32},{48,40},{56,48},{64,56},{72,6... | collective-permute-start | bytes 199688 | tf_op jit(solution)/shard_map/ppermute | solution.py:18
  19.7 11.0 %copy-start.2 = (f32[8,256]{1,0:T(8,128)S(1)}, f32[8,256]{1,0:T(8,128)}, u32[]{:S(2)}) copy-start(f32[8,256]{1,0:T(8,128)} %param.10) | copy-start | bytes 24580
  19.9 11.0 %copy-start.4 = (f32[8,256]{1,0:T(8,128)S(1)}, f32[8,256]{1,0:T(8,128)}, u32[]{:S(2)}) copy-start(f32[8,256]{1,0:T(8,128)} %param.11) | copy-start | bytes 24580
  20.2 8.2 %collective-permute-start.2 = (f32[65,10,1]{0,1,2:T(8,128)S(1)}, f32[65,10,1]{0,1,2:T(8,128)S(1)}, u32[]{:S(2)}, u32[]{:S(2)}) collective-permute-start(f32[65,10,1]{0,1,2:T(8,128)S(1)} %copy.38), channel_id=1, source_target_pairs={{0,1},{1,2},{2,3},{3,4},{4,5},{5,6},{6,7},{8,9},{9,10},{10,11},{11... | collective-permute-start | bytes 7808 | tf_op jit(solution)/shard_map/ppermute | solution.py:15
  25.4 5.0 %collective-permute-start.3 = (f32[65,10,1]{0,1,2:T(8,128)S(1)}, f32[65,10,1]{0,1,2:T(8,128)S(1)}, u32[]{:S(2)}, u32[]{:S(2)}) collective-permute-start(f32[65,10,1]{0,1,2:T(8,128)S(1)} %copy.39), channel_id=1, source_target_pairs={{1,0},{2,1},{3,2},{4,3},{5,4},{6,5},{7,6},{9,8},{10,9},{11,10},{12... | collective-permute-start | bytes 7808 | tf_op jit(solution)/shard_map/ppermute | solution.py:18
  33.4 4.3 %copy-start.6 = (s32[1,64]{1,0:T(1,128)S(1)}, s32[1,64]{1,0:T(1,128)}, u32[]{:S(2)}) copy-start(s32[1,64]{1,0:T(1,128)} %param.12) | copy-start | bytes 772
  33.4 30.6 %all-to-all-start = ((bf16[8,64,8,256]{3,2,1,0:T(8,128)(2,1)}), bf16[8,64,8,256]{3,2,1,0:T(8,128)(2,1)S(1)}, u32[]{:S(2)}, u32[]{:S(2)}) async-start(bf16[8,64,8,256]{3,2,1,0:T(8,128)(2,1)} %stack.2), calls=%async_computation | async-start | bytes 4194304 | tf_op jit(solution)/shard_map/all_to_all | solution.py:55
  37.7 97.2 %reduce-scatter.2.cloned.1.call-start = ((), (), s32[]{:S(2)}) async-start(), calls=%async_computation.2 | async-start | bytes 4718592 | tf_op jit(solution)/shard_map/reduce_scatter | solution.py:75
  72.9 2.4 copy-start.1
  72.9 3.2 %copy-start.5 = (f32[1,64]{1,0:T(1,128)S(1)}, f32[1,64]{1,0:T(1,128)}, u32[]{:S(2)}) copy-start(f32[1,64]{1,0:T(1,128)} %param.14) | copy-start | bytes 772
  136.2 21.0 %copy-start = (bf16[64,8,256]{2,1,0:T(8,128)(2,1)S(1)}, bf16[64,8,256]{2,1,0:T(8,128)(2,1)}, u32[]{:S(2)}) copy-start(bf16[64,8,256]{2,1,0:T(8,128)(2,1)} %param.8) | copy-start | bytes 786436
  136.2 21.0 %copy-start.3 = (f32[8,256]{1,0:T(8,128)S(1)}, f32[8,256]{1,0:T(8,128)}, u32[]{:S(2)}) copy-start(f32[8,256]{1,0:T(8,128)} %param.9) | copy-start | bytes 24580
  136.3 5.9 %collective-permute-start.4 = (f32[64,1,256]{2,1,0:T(1,128)S(1)}, f32[64,1,256]{2,1,0:T(1,128)S(1)}, u32[]{:S(2)}, u32[]{:S(2)}) collective-permute-start(f32[64,1,256]{2,1,0:T(1,128)S(1)} %get-tuple-element.14), channel_id=1, source_target_pairs={{8,0},{16,8},{24,16},{32,24},{40,32},{48,40},{56,48},{64,56},{72,6... | collective-permute-start | bytes 196616 | tf_op jit(solution)/shard_map/ppermute | solution.py:18
  137.6 5.3 %collective-permute-start.5 = (f32[64,1,256]{2,1,0:T(1,128)S(1)}, f32[64,1,256]{2,1,0:T(1,128)S(1)}, u32[]{:S(2)}, u32[]{:S(2)}) collective-permute-start(f32[64,1,256]{2,1,0:T(1,128)S(1)} %get-tuple-element.13), channel_id=1, source_target_pairs={{0,8},{8,16},{16,24},{24,32},{32,40},{40,48},{48,56},{56,64},{64,7... | collective-permute-start | bytes 196616 | tf_op jit(solution)/shard_map/ppermute | solution.py:15
  143.3 10.5 %collective-permute-start.6 = (f32[64,10,1]{2,1,0:T(8,128)S(1)}, f32[64,10,1]{2,1,0:T(8,128)S(1)}, u32[]{:S(2)}, u32[]{:S(2)}) collective-permute-start(f32[64,10,1]{2,1,0:T(8,128)S(1)} %get-tuple-element.9), channel_id=1, source_target_pairs={{1,0},{2,1},{3,2},{4,3},{5,4},{6,5},{7,6},{9,8},{10,9},{11,10},{12... | collective-permute-start | bytes 7688 | tf_op jit(solution)/shard_map/ppermute | solution.py:18
  149.2 8.0 %collective-permute-start.7 = (f32[64,10,1]{2,1,0:T(8,128)S(1)}, f32[64,10,1]{2,1,0:T(8,128)S(1)}, u32[]{:S(2)}, u32[]{:S(2)}) collective-permute-start(f32[64,10,1]{2,1,0:T(8,128)S(1)} %get-tuple-element.10), channel_id=1, source_target_pairs={{0,1},{1,2},{2,3},{3,4},{4,5},{5,6},{6,7},{8,9},{9,10},{10,11},{11... | collective-permute-start | bytes 7688 | tf_op jit(solution)/shard_map/ppermute | solution.py:15
Sparse Core Ops, SparseCore 0:
  88.8 45.9 reduce-scatter.1
